TPU v7x, 256 devices: a whole 4x4x8 slice. The times are simulated.
256 devices in a mesh: bulk: 16 (over y, z_hi), col: 16 (over x, z_lo, core).
Axes of the slice: x: 4, y: 4, z: 8 (z_hi: 4, z_lo: 2; z = z_hi * 2 + z_lo), core: 2. Of those that a mesh axis runs over, the one named last changes fastest.
Arguments:
- sigma_m: bfloat16 [16384, 16384], P('bulk', 'col'), may hold values from -0.046875 to 0.046875
- sigma_n: bfloat16 [16384, 16384], P('bulk', 'col'), may hold values from -0.046875 to 0.046875
- coeffs: bfloat16 [24576, 16384], P('bulk', 'col'), may hold values from -0.0390625 to 0.0390625
- s_half: bfloat16 [24576, 512], P(('bulk', 'col')), may hold values from -6 to 6
Outputs:
- updated: float32 [24576, 512], P(('bulk', 'col'))
All inputs are finite; a program needn't handle non-finite values.
Results may differ from a plain program's by a relative error of at most 0.0051.
Values may be sent and summed in bfloat16 or wider, within the bound.
A program may use at most 128 MiB of HBM per device.

v0:
```python
import jax
import jax.numpy as jnp
from jax import lax
from jax.sharding import Mesh
from jax.sharding import PartitionSpec as P

COL = ("col_0", "col_1", "col_2")
BULK_COL = ("bulk", "col_0", "col_1", "col_2")


def copy_for_each(shard, axis):
    copies = jnp.broadcast_to(shard, (lax.axis_size(axis), *shard.shape))
    return lax.all_to_all(copies, axis, split_axis=0, concat_axis=0, tiled=True)


def joined_along(pieces, dim):
    pieces = jnp.moveaxis(pieces, 0, dim)
    shape = pieces.shape
    return pieces.reshape(*shape[:dim], shape[dim] * shape[dim + 1], *shape[dim + 2 :])


def collect(shard, axis, dim):
    pieces = copy_for_each(shard, axis)
    return joined_along(pieces, dim)


def in_blocks(shard, dim, peers):
    before, after = (shard.shape[:dim], shard.shape[dim + 1 :])
    return jnp.moveaxis(shard.reshape(*before, peers, -1, *after), dim, 0)


def summed_on_arrival(shard, axis, dim):
    peers = lax.axis_size(axis)
    pieces = lax.all_to_all(in_blocks(shard, dim, peers), axis, 0, 0, tiled=True)
    return jnp.sum(pieces, axis=0)


def filled_up(lines, peers):
    spare = -len(lines) % peers
    return jnp.pad(lines, [(0, spare)] + [(0, 0)] * (lines.ndim - 1))


def total_of(shard, axes):
    lines = shard.reshape(-1, shard.shape[-1])
    own = summed_on_arrival(filled_up(lines, lax.axis_size(axes)), axes, 0)
    whole = collect(own, axes, 0)
    return whole[: len(lines)].reshape(shard.shape)


def broadcast(shard, axis, root):
    return lax.dynamic_index_in_dim(lax.all_gather(shard, axis), root, 0, keepdims=False)


def sum_in_two_steps(shard, axes, dim):
    far, near = axes
    own = summed_on_arrival(in_blocks(shard, dim, lax.axis_size(far)), near, dim + 1)
    return jnp.sum(lax.all_to_all(own, far, 0, 0, tiled=True), axis=0)


def gather_axes(shard, axes, dim):
    far, near = axes
    initial = copy_for_each(shard, far)
    pieces = jnp.swapaxes(copy_for_each(initial, near), 0, 1)
    return joined_along(pieces.reshape(-1, *shard.shape), dim)


def nested_sum(shard, axes):
    lines = shard.reshape(-1, shard.shape[-1])
    own = sum_in_two_steps(
        filled_up(lines, lax.axis_size(axes[0]) * lax.axis_size(axes[1])), axes, 0
    )
    whole = gather_axes(own, axes, 0)
    return whole[: len(lines)].reshape(shard.shape)


def shards(sigma_m, sigma_n, coeffs, s_half):
    per_col = lax.axis_size("bulk") // lax.axis_size(COL)
    bulk_index = lax.axis_index("bulk")
    col_index = lax.axis_index(COL)
    coef_rows = coeffs
    partial_proj = lax.dot_general(
        coef_rows,
        collect(s_half, COL, 0),
        (((0,), (0,)), ((), ())),
        preferred_element_type=jnp.float32,
    )
    proj_col = total_of(partial_proj, "bulk").astype(jnp.bfloat16)
    proj_row = broadcast(proj_col, COL, bulk_index // per_col)
    mixed = (0.5 * (sigma_m.astype(jnp.float32) + sigma_n.astype(jnp.float32))).astype(jnp.bfloat16)
    row_term = jnp.dot(mixed, proj_col, preferred_element_type=jnp.float32)
    col_term = lax.dot_general(
        mixed, proj_row, (((0,), (0,)), ((), ())), preferred_element_type=jnp.float32
    )
    row_summed = nested_sum(row_term, (("col_0", "col_1"), "col_2"))
    on_block = (bulk_index // per_col == col_index).astype(jnp.float32)
    placed = row_summed * on_block
    summed = total_of(col_term + placed, "bulk")
    rotated = (0.5 * summed).astype(jnp.bfloat16)
    coef_rows = coeffs
    return sum_in_two_steps(
        jnp.dot(coef_rows, rotated, preferred_element_type=jnp.float32),
        (("col_0", "col_1"), "col_2"),
        0,
    )


def solution(mesh):
    finer = Mesh(
        mesh.devices.reshape(mesh.shape["bulk"], 4, 2, 2), ("bulk", "col_0", "col_1", "col_2")
    )
    in_specs = (P("bulk", COL), P("bulk", COL), P("bulk", COL), P(BULK_COL, None))
    out_specs = P(BULK_COL, None)
    return jax.shard_map(
        shards, mesh=finer, in_specs=in_specs, out_specs=out_specs, check_vma=False
    )
```

profile of v0, /device:TPU:1, one launch (start us, length us, event | category | flops | bytes accessed | tf_op | source)
XLA Modules:
  0.0 411.1 jit_solution(5589816779138650802)
XLA Ops:
  6.5 2.4 broadcast_in_dim.15
  8.9 7.4 %all-to-all-start = ((bf16[16,96,512]{2,1,0:T(8,128)(2,1)}), bf16[16,96,512]{2,1,0:T(8,128)(2,1)}, u32[]{:S(2)}, u32[]{:S(2)}) async-start(bf16[16,96,512]{2,1,0:T(8,128)(2,1)} %broadcast_in_dim.15), calls=%async_computation | async-start | bytes 3145728 | tf_op jit(solution)/shard_map/all_to_all | solution.py:13
  16.3 0.0 all-gather.2.cloned.1.call-start
  16.3 0.0 copy-done.1
  16.3 3.0 copy.13
  19.3 18.7 %all-to-all-done = bf16[16,96,512]{2,1,0:T(8,128)(2,1)} async-done(((bf16[16,96,512]{2,1,0:T(8,128)(2,1)}), bf16[16,96,512]{2,1,0:T(8,128)(2,1)}, u32[]{:S(2)}, u32[]{:S(2)}) %all-to-all-start) | async-done | bytes 1572896 | tf_op jit(solution)/shard_map/all_to_all | solution.py:13
  38.0 4.1 %fusion.3 = f32[16,64,512]{2,1,0:T(8,128)S(1)} fusion(bf16[16,64,1536]{2,1,0:T(8,128)(2,1)} %bitcast.39, bf16[1536,512,1]{1,0,2:T(8,128)(2,1)} %bitcast.3), kind=kOutput, calls=%fused_computation.9 | convolution fusion | flops 1610612736 | bytes 6815744 | tf_op jit(solution)/shard_map/dot_general | solution.py:81
  42.1 55.3 %all_to_all.55 = f32[16,64,512]{2,1,0:T(8,128)S(1)} all-to-all(f32[16,64,512]{2,1,0:T(8,128)S(1)} %fusion.3), channel_id=1, replica_groups=mesh['bulk'=16,'col_0'=4,'col_1'=2,'col_2'=2] {'bulk'}, dimensions={0} | all-to-all | bytes 4194304 | tf_op jit(solution)/shard_map/all_to_all | solution.py:34
  97.4 0.2 reduce_sum.54
  97.6 0.0 copy-start.3
  97.6 0.1 broadcast_in_dim.16
  97.7 22.9 %all_to_all.56 = bf16[16,64,512]{2,1,0:T(8,128)(2,1)} all-to-all(bf16[16,64,512]{2,1,0:T(8,128)(2,1)S(1)} %broadcast_in_dim.16), channel_id=1, replica_groups=mesh['bulk'=16,'col_0'=4,'col_1'=2,'col_2'=2] {'bulk'}, dimensions={0} | all-to-all | bytes 2097152 | tf_op jit(solution)/shard_map/all_to_all | solution.py:13
  120.6 0.0 all-gather.2.cloned.1.call-update
  120.6 0.0 copy-done.3
  120.6 0.0 copy-start
  120.6 2.6 multiply_convert_fusion
  123.3 0.0 copy-start.4
  123.3 0.0 copy-done
  123.3 1.2 convolution_bitcast_fusion.1
  124.5 0.1 copy-done.4
  124.6 0.2 copy.14
  124.9 12.0 %all_to_all.57 = f32[2,8,64,512]{3,2,1,0:T(8,128)S(1)} all-to-all(f32[2,8,64,512]{3,2,1,0:T(8,128)S(1)} %copy.14), channel_id=1, replica_groups=mesh['bulk'=16,'col_0'=4,'col_1'=2,'col_2'=2] {'col_2'}, dimensions={0} | all-to-all | bytes 4194304 | tf_op jit(solution)/shard_map/all_to_all | solution.py:34
  136.9 0.3 reduce_sum.55
  137.2 39.1 %all_to_all.58 = f32[8,64,512]{2,1,0:T(8,128)S(1)} all-to-all(f32[8,64,512]{2,1,0:T(8,128)S(1)} %reduce_sum.55), channel_id=1, replica_groups=mesh['bulk'=16,'col_0'=4,'col_1'=2,'col_2'=2] {'col_0','col_1'}, dimensions={0} | all-to-all | bytes 2097152 | tf_op jit(solution)/shard_map/all_to_all | solution.py:57
  176.3 0.1 reduce_sum.56
  176.4 1.1 broadcast_in_dim.17
  177.5 3.6 all-to-all-start.5
  181.1 26.8 %all-to-all-done.5 = f32[8,64,512]{2,1,0:T(8,128)S(1)} async-done(((f32[8,64,512]{2,1,0:T(8,128)}), f32[8,64,512]{2,1,0:T(8,128)S(1)}, u32[]{:S(2)}, u32[]{:S(2)}) %all-to-all-start.5) | async-done | bytes 1048608 | tf_op jit(solution)/shard_map/all_to_all | solution.py:13
  207.9 0.2 broadcast_in_dim.18
  208.2 7.5 %all_to_all.59 = f32[2,8,64,512]{3,2,1,0:T(8,128)S(1)} all-to-all(f32[2,8,64,512]{3,2,1,0:T(8,128)S(1)} %broadcast_in_dim.18), channel_id=1, replica_groups=mesh['bulk'=16,'col_0'=4,'col_1'=2,'col_2'=2] {'col_2'}, dimensions={0} | all-to-all | bytes 4194304 | tf_op jit(solution)/shard_map/all_to_all | solution.py:13
  215.6 0.2 multiply_bitcast_fusion
  215.9 0.0 copy-start.5
  215.9 1.5 copy.15
  217.4 28.4 %all-gather.2.cloned.1.call-done = bf16[16,1024,512]{2,1,0:T(8,128)(2,1)} async-done(((bf16[1,1024,512]{2,1,0:T(8,128)(2,1)}), bf16[16,1024,512]{2,1,0:T(8,128)(2,1)}) %all-gather.2.cloned.1.call-update) | async-done | bytes 16777232 | tf_op jit(solution)/shard_map/all_gather | solution.py:51
  245.8 3.2 bitcast_add_fusion
  249.0 60.2 %all_to_all.60 = f32[16,64,512]{2,1,0:T(8,128)S(1)} all-to-all(f32[16,64,512]{2,1,0:T(8,128)S(1)} %bitcast.41), channel_id=1, replica_groups=mesh['bulk'=16,'col_0'=4,'col_1'=2,'col_2'=2] {'bulk'}, dimensions={0} | all-to-all | bytes 4194304 | tf_op jit(solution)/shard_map/all_to_all | solution.py:34
  309.3 0.2 reduce_sum.57
  309.4 0.3 broadcast_in_dim.19
  309.7 51.8 %all_to_all.61 = f32[16,64,512]{2,1,0:T(8,128)S(1)} all-to-all(f32[16,64,512]{2,1,0:T(8,128)S(1)} %broadcast_in_dim.19), channel_id=1, replica_groups=mesh['bulk'=16,'col_0'=4,'col_1'=2,'col_2'=2] {'bulk'}, dimensions={0} | all-to-all | bytes 4194304 | tf_op jit(solution)/shard_map/all_to_all | solution.py:13
  361.5 0.3 multiply_convert_fusion.1
  361.8 1.6 copy-done.2
  363.4 3.5 convolution_bitcast_fusion
  366.9 2.4 copy.16
  369.3 0.3 copy.17
  369.6 6.4 %all_to_all.62 = f32[2,8,96,512]{3,2,1,0:T(8,128)S(1)} all-to-all(f32[2,8,96,512]{3,2,1,0:T(8,128)S(1)} %copy.17), channel_id=1, replica_groups=mesh['bulk'=16,'col_0'=4,'col_1'=2,'col_2'=2] {'col_2'}, dimensions={0} | all-to-all | bytes 6291456 | tf_op jit(solution)/shard_map/all_to_all | solution.py:34
  376.0 1.6 reduce_sum.58
  377.6 25.9 %all_to_all.63 = f32[8,96,512]{2,1,0:T(8,128)S(1)} all-to-all(f32[8,96,512]{2,1,0:T(8,128)} %reduce_sum.58), channel_id=1, replica_groups=mesh['bulk'=16,'col_0'=4,'col_1'=2,'col_2'=2] {'col_0','col_1'}, dimensions={0} | all-to-all | bytes 3145728 | tf_op jit(solution)/shard_map/all_to_all | solution.py:57
  403.5 0.8 reduce_sum.59
  (3 shorter events, 0.0 us)
Async XLA Ops:
  6.5 9.8 %copy-start.1 = (bf16[1536,1024]{1,0:T(8,128)(2,1)S(1)}, bf16[1536,1024]{1,0:T(8,128)(2,1)}, u32[]{:S(2)}) copy-start(bf16[1536,1024]{1,0:T(8,128)(2,1)} %param.6) | copy-start | bytes 9437188
  8.9 29.1 %all-to-all-start = ((bf16[16,96,512]{2,1,0:T(8,128)(2,1)}), bf16[16,96,512]{2,1,0:T(8,128)(2,1)}, u32[]{:S(2)}, u32[]{:S(2)}) async-start(bf16[16,96,512]{2,1,0:T(8,128)(2,1)} %broadcast_in_dim.15), calls=%async_computation | async-start | bytes 3145728 | tf_op jit(solution)/shard_map/all_to_all | solution.py:13
  16.3 229.5 %all-gather.2.cloned.1.call-start = ((), (), s32[]{:S(2)}) async-start(), calls=%async_computation.11 | async-start | bytes 17825792 | tf_op jit(solution)/shard_map/all_gather | solution.py:51
  97.6 23.0 %copy-start.3 = (bf16[1024,1024]{1,0:T(8,128)(2,1)S(1)}, bf16[1024,1024]{1,0:T(8,128)(2,1)}, u32[]{:S(2)}) copy-start(bf16[1024,1024]{1,0:T(8,128)(2,1)} %param.5) | copy-start | bytes 6291460
  120.6 2.7 copy-start
  123.3 1.4 copy-start.4
  177.5 30.4 %all-to-all-start.5 = ((f32[8,64,512]{2,1,0:T(8,128)}), f32[8,64,512]{2,1,0:T(8,128)S(1)}, u32[]{:S(2)}, u32[]{:S(2)}) async-start(f32[8,64,512]{2,1,0:T(8,128)} %broadcast_in_dim.17), calls=%async_computation.5 | async-start | bytes 2097152 | tf_op jit(solution)/shard_map/all_to_all | solution.py:13
  215.9 29.9 %copy-start.5 = (bf16[1024,1024]{1,0:T(8,128)(2,1)S(1)}, bf16[1024,1024]{1,0:T(8,128)(2,1)}, u32[]{:S(2)}) copy-start(bf16[1024,1024]{1,0:T(8,128)(2,1)} %copy-done.4) | copy-start | bytes 6291460
  361.5 1.9 copy-start.2
Sparse Core Ops, SparseCore 0:
  120.7 125.0 all-gather.1
where the time goes:
time: 412 us; the launch traced here: 411 us
  blocking collectives  281 us (68%)
  waiting for transfers between devices  73.9 us (18%)
  between operations  13.6 us (3%)
  local copies, waits for them, and re-layouts  13.2 us (3%)
  matrix products  12.1 us (3%)
  starting transfers between devices  11 us (3%)
  other arithmetic  6.27 us (2%)
    all_to_all x4, blocking collectives, summed_on_arrival(): lax.all_to_all(in_blocks(shard, dim, peers), axis, 0, 0, tiled=True)  134 us
    all_to_all x3, blocking collectives, copy_for_each(): return lax.all_to_all(copies, axis, split_axis=0, concat_axis=0, tiled=True)  82.2 us
    all_to_all x2, blocking collectives, sum_in_two_steps(): return jnp.sum(lax.all_to_all(own, far, 0, 0, tiled=True), axis=0)  65 us
    all_to_all x2, waiting for transfers between devices, copy_for_each(): return lax.all_to_all(copies, axis, split_axis=0, concat_axis=0, tiled=True)  45.5 us
    all_gather x1, waiting for transfers between devices, broadcast(): lax.all_gather(shard, axis)  28.4 us
    all_to_all x2, starting transfers between devices, copy_for_each(): return lax.all_to_all(copies, axis, split_axis=0, concat_axis=0, tiled=True)  11 us
  transfers between devices with their start and end apart: 3, of which 3 were waited for; matrix products, arithmetic and copies ran while one was open for 3% of the time, Pallas kernels for 0%

commit v1 on v0

v1 whole, which is shorter than its diff:
```python
import jax
import jax.numpy as jnp
from jax import lax
from jax.experimental import pallas as pl
from jax.experimental.pallas import tpu as pltpu
from jax.sharding import PartitionSpec as P

BF, F32 = jnp.bfloat16, jnp.float32
GROUPS, LANES = 4, 128
CHUNKS = 2
SLOTS = ((0, 2, 3, 1), (0, 1, 2, 3))


def place(colour, v):
    if colour == 0:
        return ((v + 1) // 2) % 2, v // 2
    return v // 2, v % 2


def partners(colour, v):
    near, far = v + 1 - 2 * (v % 2), 3 - v
    return (near, far) if colour == 0 else (far, near)


def dot(a, b, da, db):
    return lax.dot_general(a, b, (((da,), (db,)), ((), ())), preferred_element_type=F32)


def kernel(sm_hbm, sn_hbm, co_hbm, s_ref, o_ref, bufs, sems):
    b, c = lax.axis_index("bulk"), lax.axis_index("col")
    y, h = b // 4, b % 4
    x, l, k = c // 4, (c // 2) % 2, c % 2
    hl, hk = h // 2, h % 2

    def dev(y=y, h=h, x=x, l=l, k=k):
        return {"bulk": y * 4 + h, "col": x * 4 + l * 2 + k}

    flipped = {"bulk": c, "col": b}
    B, S = bufs, sems
    pending = []

    loads = [
        pltpu.make_async_copy(src, dst, S["load"].at[i])
        for i, (src, dst) in enumerate(
            ((sm_hbm, B["sm"]), (sn_hbm, B["sn"]), (co_hbm, B["co"]))
        )
    ]
    for ld in loads:
        ld.start()

    bar = pltpu.get_barrier_semaphore()
    shifts = [(dx, dl) for dx in range(4) for dl in range(2) if dx or dl]
    peers = [dev(x=(x + dx) % 4, l=(l + dl) % 2) for dx, dl in shifts]
    greeted = peers + [dev(k=1 - k), dev(y=y + 1 - 2 * (y % 2)), dev(y=3 - y)]
    greeted += [dev(h=(h + j) % 4) for j in (1, 2, 3)]
    greeted += [flipped]
    for to in greeted:
        pl.semaphore_signal(bar, inc=1, device_id=to)

    for p in range(CHUNKS):
        B["sg"][p, x, l, k] = s_ref[:, p * 256 : (p + 1) * 256]

    pl.semaphore_wait(bar, len(greeted))

    def send(src, dst, sem, at, to):
        cp = pltpu.make_async_remote_copy(
            src_ref=src,
            dst_ref=dst,
            send_sem=S[sem].at[(0, *at)],
            recv_sem=S[sem].at[(1, *at)],
            device_id=to,
        )
        cp.start()
        pending.append(cp)
        return cp

    own_s = [B["sg"].at[p, x, l, k] for p in range(CHUNKS)]
    arrive = [
        [send(own_s[p], own_s[p], "a", (p, j), to) for j, to in enumerate(peers)]
        for p in range(CHUNKS)
    ]
    across = [
        [send(own_s[p], own_s[p], "ac", (p, 7), dev(k=1 - k))] for p in range(CHUNKS)
    ]

    loads[0].wait()
    loads[1].wait()

    def mix(i, _):
        r = pl.ds(pl.multiple_of(i * 64, 64), 64)
        total = B["sm"][r, :].astype(F32) + B["sn"][r, :].astype(F32)
        B["mx"][r, :] = (0.5 * total).astype(BF)
        return 0

    lax.fori_loop(0, 16, mix, 0)
    loads[2].wait()

    def split_rows(name, p, value, rows):
        for i in range(2):
            part = value[:, i * LANES : (i + 1) * LANES]
            B[name][2 * p + i] = part.reshape(4, 2, 2, rows, LANES)

    def joined(name, p):
        return jnp.concatenate(
            [B[name][2 * p + i].reshape(-1, LANES) for i in range(2)], axis=1
        )

    def bulk_sum_1(n, g):
        half, _ = place(g % 2, y)
        B[n + "_s1"][g] = B[n][g, pl.ds(2 * (1 - half), 2)].astype(BF)
        to = dev(y=partners(g % 2, y)[0])
        return send(B[n + "_s1"].at[g], B[n + "_r1"].at[g], n + "_1", (g,), to)

    def bulk_sum_2(n, g, cp):
        cp.wait_recv()
        half, quart = place(g % 2, y)
        f, r1 = B[n], B[n + "_r1"]
        other = f[g, 2 * half + 1 - quart] + r1[g, 1 - quart].astype(F32)
        B[n + "_s2"][g] = other.astype(BF)
        to = dev(y=partners(g % 2, y)[1])
        cp = send(B[n + "_s2"].at[g], B[n + "_r2"].at[g], n + "_2", (g,), to)
        f[g, 2 * half + quart] = f[g, 2 * half + quart] + r1[g, quart].astype(F32)
        return cp

    def bulk_sum_3(n, g, cp):
        cp.wait_recv()
        half, quart = place(g % 2, y)
        total = B[n][g, 2 * half + quart] + B[n + "_r2"][g].astype(F32)
        B[n + "_s3"][g] = total.astype(B[n + "_s3"].dtype)
        cps = []
        for j in (1, 2, 3):
            to = (h + j) % 4
            cps.append(
                send(
                    B[n + "_s3"].at[g, to // 2, to % 2],
                    B[n + "_r3"].at[g, j - 1],
                    n + "_3",
                    (g, j - 1),
                    dev(h=to),
                )
            )
        own = B[n][g, 2 * half + quart, hl, hk]
        B[n + "_own"][g] = own + B[n + "_r2"][g, hl, hk].astype(F32)
        return cps

    def bulk_sum_end(n, g, cps):
        for cp in cps:
            cp.wait_recv()
        r3 = B[n + "_r3"]
        total = B[n + "_own"][g] + r3[g, 0].astype(F32)
        return total + (r3[g, 1].astype(F32) + r3[g, 2].astype(F32))

    def bulk_gather_1(n, g):
        half, quart = place(g % 2, y)
        piece = B[n].at[g, 2 * half + quart, hl, hk]
        return [
            send(piece, piece, n + "_g1", (g, j - 1), dev(h=(h + j) % 4))
            for j in (1, 2, 3)
        ]

    def bulk_gather_2(n, g, cps):
        for cp in cps:
            cp.wait_recv()
        half, quart = place(g % 2, y)
        piece = B[n].at[g, 2 * half + quart]
        return send(piece, piece, n + "_g2", (g,), dev(y=partners(g % 2, y)[1]))

    def bulk_gather_3(n, g, cp):
        cp.wait_recv()
        half, _ = place(g % 2, y)
        piece = B[n].at[g, pl.ds(2 * half, 2)]
        return send(piece, piece, n + "_g3", (g,), dev(y=partners(g % 2, y)[0]))

    def col_sum_1(n, g):
        return send(
            B[n].at[g, :, :, 1 - k], B[n + "_r1"].at[g], n + "_1", (g,), dev(k=1 - k)
        )

    def col_sum_2(n, g, cp):
        cp.wait_recv()
        half, _ = place(g % 2, x)
        f, r1, away = B[n], B[n + "_r1"], pl.ds(2 * (1 - half), 2)
        out = f[g, away, :, k] + r1[g, away]
        B[n + "_s2"][g] = out.astype(B[n + "_s2"].dtype)
        to = dev(x=partners(g % 2, x)[0])
        cp = send(B[n + "_s2"].at[g], B[n + "_r2"].at[g], n + "_2", (g,), to)
        here = pl.ds(2 * half, 2)
        B[n + "_h"][g] = f[g, here, :, k] + r1[g, here]
        return cp

    def col_sum_3(n, g, cp):
        cp.wait_recv()
        _, quart = place(g % 2, x)
        f, r2 = B[n + "_h"], B[n + "_r2"]
        out = f[g, 1 - quart] + r2[g, 1 - quart].astype(F32)
        B[n + "_s3"][g] = out.astype(B[n + "_s3"].dtype)
        to = dev(x=partners(g % 2, x)[1])
        cp = send(B[n + "_s3"].at[g], B[n + "_r3"].at[g], n + "_3", (g,), to)
        B[n + "_q"][g] = f[g, quart] + r2[g, quart].astype(F32)
        return cp

    def col_sum_4(n, g, cp):
        cp.wait_recv()
        f, r3 = B[n + "_q"], B[n + "_r3"]
        out = f[g, 1 - l] + r3[g, 1 - l].astype(F32)
        B[n + "_s4"][g] = out.astype(B[n + "_s4"].dtype)
        return send(
            B[n + "_s4"].at[g], B[n + "_r4"].at[g], n + "_4", (g,), dev(l=1 - l)
        )

    def col_sum_end(n, g, cp):
        cp.wait_recv()
        f, r3 = B[n + "_q"], B[n + "_r3"]
        return f[g, l] + r3[g, l].astype(F32) + B[n + "_r4"][g].astype(F32)

    def flip(src, dst, sem, g):
        cp = pltpu.make_async_remote_copy(
            src_ref=src,
            dst_ref=dst,
            send_sem=S[sem].at[0, g],
            recv_sem=S[sem].at[1, g],
            device_id=flipped,
        )

        @pl.when(b != c)
        def _():
            cp.start()

        @pl.when(b == c)
        def _():
            dst[...] = src[...]

        return cp

    def flip_wait(cp):
        @pl.when(b != c)
        def _():
            cp.wait()

    def col_gather_1(n, g, cp):
        flip_wait(cp)
        half, quart = place(g % 2, x)
        piece = B[n].at[g, 2 * half + quart, l, k]
        return send(piece, piece, n + "_g1", (g,), dev(l=1 - l))

    def col_gather_2(n, g, cp):
        cp.wait_recv()
        half, quart = place(g % 2, x)
        piece = B[n].at[g, 2 * half + quart, :, k]
        return send(piece, piece, n + "_g2", (g,), dev(x=partners(g % 2, x)[1]))

    def col_gather_3(n, g, cp):
        cp.wait_recv()
        half, _ = place(g % 2, x)
        piece = B[n].at[g, pl.ds(2 * half, 2), :, k]
        return send(piece, piece, n + "_g3", (g,), dev(x=partners(g % 2, x)[0]))

    def col_gather_4(n, g, cp):
        cp.wait_recv()
        piece = B[n].at[g, :, :, k]
        return send(piece, piece, n + "_g4", (g,), dev(k=1 - k))

    groups = range(GROUPS)
    of_chunk = [(2 * p, 2 * p + 1) for p in range(CHUNKS)]

    cp = {}
    for p in range(CHUNKS):
        for j, (dx, dl) in enumerate(shifts):
            arrive[p][j].wait_recv()
            block = B["sg"].at[p, (x - dx + 4) % 4, (l - dl + 2) % 2, k]
            across[p].append(send(block, block, "ac", (p, j), dev(k=1 - k)))
        for one in across[p]:
            one.wait_recv()
        rows = B["sg"][p].reshape(-1, 2 * LANES)
        split_rows("fp", p, dot(B["co"][...], rows, 0, 0), 64)
        for g in of_chunk[p]:
            cp[g] = bulk_sum_1("fp", g)
    for g in groups:
        cp[g] = bulk_sum_2("fp", g, cp[g])
    for g in groups:
        cp[g] = bulk_sum_3("fp", g, cp[g])
    near, far = {}, {}
    for g in groups:
        half, quart = place(g % 2, y)
        at = (g, 2 * half + quart, hl, hk)
        B["pc"][at] = bulk_sum_end("fp", g, cp[g]).astype(BF)
        near[g] = bulk_gather_1("pc", g)
        far[g] = flip(B["pc"].at[at], B["pr"].at[at], "pr_t", g)

    for g in groups:
        far[g] = col_gather_1("pr", g, far[g])
    for g in groups:
        near[g] = bulk_gather_2("pc", g, near[g])
    for g in groups:
        far[g] = col_gather_2("pr", g, far[g])
    for g in groups:
        near[g] = bulk_gather_3("pc", g, near[g])
    for g in groups:
        far[g] = col_gather_3("pr", g, far[g])
    for g in groups:
        far[g] = col_gather_4("pr", g, far[g])
    row, col = {}, {}
    for p in range(CHUNKS):
        for g in of_chunk[p]:
            near[g].wait_recv()
        split_rows("fr", p, dot(B["mx"][...], joined("pc", p), 1, 0), 64)
        for g in of_chunk[p]:
            row[g] = col_sum_1("fr", g)
        for g in of_chunk[p]:
            far[g].wait_recv()
        split_rows("fc", p, dot(B["mx"][...], joined("pr", p), 0, 0), 64)
        for g in of_chunk[p]:
            col[g] = bulk_sum_1("fc", g)

    for g in groups:
        row[g] = col_sum_2("fr", g, row[g])
    for g in groups:
        col[g] = bulk_sum_2("fc", g, col[g])
    for g in groups:
        row[g] = col_sum_3("fr", g, row[g])
    for g in groups:
        col[g] = bulk_sum_3("fc", g, col[g])
    for g in groups:
        row[g] = col_sum_4("fr", g, row[g])
    for g in groups:
        B["fr_t"][g] = col_sum_end("fr", g, row[g])
        row[g] = flip(B["fr_t"].at[g], B["fr_u"].at[g], "fr_t", g)
    for g in groups:
        total = bulk_sum_end("fc", g, col[g])
        flip_wait(row[g])
        half, quart = place(g % 2, y)
        rotated = (0.5 * (total + B["fr_u"][g])).astype(BF)
        B["ro"][g, 2 * half + quart, hl, hk] = rotated
        near[g] = bulk_gather_1("ro", g)
    for g in groups:
        near[g] = bulk_gather_2("ro", g, near[g])
    for g in groups:
        near[g] = bulk_gather_3("ro", g, near[g])

    for p in range(CHUNKS):
        for g in of_chunk[p]:
            near[g].wait_recv()
        value = dot(B["co"][...], joined("ro", p), 1, 0)
        for g in of_chunk[p]:
            i = g % 2
            part = value[:, i * LANES : (i + 1) * LANES].reshape(4, 2, 2, 96, LANES)
            for v in range(4):
                B["fu"][g, SLOTS[i][v]] = part[v]
            row[g] = col_sum_1("fu", g)
    for g in groups:
        row[g] = col_sum_2("fu", g, row[g])
    for g in groups:
        row[g] = col_sum_3("fu", g, row[g])
    for g in groups:
        row[g] = col_sum_4("fu", g, row[g])
    for g in groups:
        o_ref[:, g * LANES : (g + 1) * LANES] = col_sum_end("fu", g, row[g])
    for one in pending:
        one.wait_send()


def scratch():
    V = pltpu.VMEM

    def bulk(n, z):
        return {
            n: V((GROUPS, 4, 2, 2, 64, LANES), F32),
            n + "_s1": V((GROUPS, 2, 2, 2, 64, LANES), BF),
            n + "_r1": V((GROUPS, 2, 2, 2, 64, LANES), BF),
            n + "_s2": V((GROUPS, 2, 2, 64, LANES), BF),
            n + "_r2": V((GROUPS, 2, 2, 64, LANES), BF),
            n + "_s3": V((GROUPS, 2, 2, 64, LANES), z),
            n + "_r3": V((GROUPS, 3, 64, LANES), z),
            n + "_own": V((GROUPS, 64, LANES), F32),
        }

    def col(n, rows, two, three, four):
        return {
            n: V((GROUPS, 4, 2, 2, rows, LANES), F32),
            n + "_r1": V((GROUPS, 4, 2, rows, LANES), F32),
            n + "_h": V((GROUPS, 2, 2, rows, LANES), F32),
            n + "_s2": V((GROUPS, 2, 2, rows, LANES), two),
            n + "_r2": V((GROUPS, 2, 2, rows, LANES), two),
            n + "_q": V((GROUPS, 2, rows, LANES), F32),
            n + "_s3": V((GROUPS, 2, rows, LANES), three),
            n + "_r3": V((GROUPS, 2, rows, LANES), three),
            n + "_s4": V((GROUPS, rows, LANES), four),
            n + "_r4": V((GROUPS, rows, LANES), four),
        }

    whole = (GROUPS, 4, 2, 2, 64, LANES)
    bufs = {
        "sm": V((1024, 1024), BF),
        "sn": V((1024, 1024), BF),
        "mx": V((1024, 1024), BF),
        "co": V((1536, 1024), BF),
        "sg": V((CHUNKS, 4, 2, 2, 96, 2 * LANES), BF),
        "pc": V(whole, BF),
        "pr": V(whole, BF),
        "ro": V(whole, BF),
        "fr_t": V((GROUPS, 64, LANES), F32),
        "fr_u": V((GROUPS, 64, LANES), F32),
        **bulk("fp", BF),
        **bulk("fc", BF),
        **col("fr", 64, F32, F32, F32),
        **col("fu", 96, BF, BF, BF),
    }
    D = pltpu.SemaphoreType.DMA
    sems = {"load": D((3,)), "a": D((2, CHUNKS, 7)), "ac": D((2, CHUNKS, 8))}
    for n in ("fp", "fc"):
        sems.update({n + "_1": D((2, GROUPS)), n + "_2": D((2, GROUPS))})
        sems[n + "_3"] = D((2, GROUPS, 3))
    for n in ("pc", "ro"):
        sems.update({n + "_g2": D((2, GROUPS)), n + "_g3": D((2, GROUPS))})
        sems[n + "_g1"] = D((2, GROUPS, 3))
    for i in range(1, 5):
        for n in ("fr_", "fu_", "pr_g"):
            sems[n + str(i)] = D((2, GROUPS))
    sems["pr_t"] = D((2, GROUPS))
    sems["fr_t"] = D((2, GROUPS))
    return bufs, sems


def shards(sigma_m, sigma_n, coeffs, s_half):
    bufs, sems = scratch()
    names, sem_names = list(bufs), list(sems)

    def body(*refs):
        rest = refs[5:]
        return kernel(
            *refs[:5],
            dict(zip(names, rest[: len(names)])),
            dict(zip(sem_names, rest[len(names) :])),
        )

    hbm, vmem = pl.BlockSpec(memory_space=pl.ANY), pl.BlockSpec(memory_space=pltpu.VMEM)
    return pl.pallas_call(
        body,
        out_shape=jax.ShapeDtypeStruct(s_half.shape, F32),
        in_specs=[hbm, hbm, hbm, vmem],
        out_specs=vmem,
        scratch_shapes=[*bufs.values(), *sems.values()],
        compiler_params=pltpu.CompilerParams(
            collective_id=0, has_side_effects=True, vmem_limit_bytes=60 << 20
        ),
        name="gw_update",
    )(sigma_m, sigma_n, coeffs, s_half)


def solution(mesh):
    in_specs = (P("bulk", "col"),) * 3 + (P(("bulk", "col"), None),)
    return jax.shard_map(
        shards,
        mesh=mesh,
        in_specs=in_specs,
        out_specs=P(("bulk", "col"), None),
        check_vma=False,
    )
```

time: 412 us -> 125 us (0.30)
  blocking collectives: 281 us -> 0 us
  Pallas kernels: 0 us -> 124 us
  waiting for transfers between devices: 73.9 us -> 0 us
  between operations: 13.6 us -> 0.01 us
  matrix products: 12.1 us -> 0 us
  local copies, waits for them, and re-layouts: 13.2 us -> 1.62 us
  starting transfers between devices: 11 us -> 0 us
  other arithmetic: 6.27 us -> 0 us
    all_to_all x9 -> x0, blocking collectives: 281 us -> none  [the longest x4 134 us: summed_on_arrival(): lax.all_to_all(in_blocks(shard, dim, peers), axis, 0, 0, tiled=True)]
    pallas_call x0 -> x1, Pallas kernels: none -> 124 us  [shards(): pl.pallas_call(body, out_shape=jax.ShapeDtypeStruct(s_half.shape, F32), i...]
    all_to_all x2 -> x0, waiting for transfers between devices: 45.5 us -> none  [copy_for_each(): return lax.all_to_all(copies, axis, split_axis=0, concat_axis=0, tiled=True)]
    all_gather x1 -> x0, waiting for transfers between devices: 28.4 us -> none  [broadcast(): lax.all_gather(shard, axis)]
    dot_general x4 -> x0, matrix products: 12.1 us -> none  [the longest x1 4.13 us: shards(): lax.dot_general(coef_rows, collect(s_half, COL, 0), (((0,), (0,)), ((), (...]
    all_to_all x2 -> x0, starting transfers between devices: 11 us -> none  [copy_for_each(): return lax.all_to_all(copies, axis, split_axis=0, concat_axis=0, tiled=True)]
  transfers between devices with their start and end apart: 3 -> 0, of which waited for: 3 -> 0; matrix products, arithmetic and copies ran while one was open for 3% -> 0% of each run, Pallas kernels for 0% -> 0%
where the time goes in v1:
time: 125 us
  Pallas kernels  124 us (99%)
  local copies, waits for them, and re-layouts  1.62 us (1%)
    pallas_call x1, Pallas kernels, shards(): pl.pallas_call(body, out_shape=jax.ShapeDtypeStruct(s_half.shape, F32), i...  124 us

profile of v1, /device:TPU:1, one launch (start us, length us, event | category | flops | bytes accessed | tf_op | source)
XLA Modules:
  0.0 125.2 jit_solution(16648650368858448838)
XLA Ops:
  0.0 123.6 %gw_update.1 = f32[96,512]{1,0:T(8,128)} custom-call(bf16[1024,1024]{1,0:T(8,128)(2,1)} %refs_0_.1, bf16[1024,1024]{1,0:T(8,128)(2,1)} %refs_1_.1, bf16[1536,1024]{1,0:T(8,128)(2,1)} %refs_2_.1, bf16[96,512]{1,0:T(8,128)(2,1)} %refs_3_.1), custom_call_target="tpu_custom_call" | custom-call | tf_op jit(solution)/shard_map/gw_update/pallas_call | solution.py:437
  123.6 1.6 %copy.6 = f32[96,512]{1,0:T(8,128)} copy(f32[96,512]{1,0:T(8,128)} %gw_update.1) | data formatting | bytes 393216

commit v2 on v1

--- a/solution.py
+++ b/solution.py
@@ -35,9 +35,16 @@
     def dev(y=y, h=h, x=x, l=l, k=k):
         return {"bulk": y * 4 + h, "col": x * 4 + l * 2 + k}
 
-    flipped = {"bulk": c, "col": b}
+    w = 2 * l + k
+    v, u = (y - x + 4) % 4, (h - w + 4) % 4
+    ul, uk = u // 2, u % 2
+
+    flip_to = {"bulk": c, "col": ((x - y + 4) % 4) * 4 + (w - h + 4) % 4}
+    flip_back = {"bulk": v * 4 + u, "col": b}
+
+    fixed = (b == 0) & (c == 0)
     B, S = bufs, sems
-    pending = []
+    pending, pending_flips = [], []
 
     loads = [
         pltpu.make_async_copy(src, dst, S["load"].at[i])
@@ -53,7 +60,7 @@
     peers = [dev(x=(x + dx) % 4, l=(l + dl) % 2) for dx, dl in shifts]
     greeted = peers + [dev(k=1 - k), dev(y=y + 1 - 2 * (y % 2)), dev(y=3 - y)]
     greeted += [dev(h=(h + j) % 4) for j in (1, 2, 3)]
-    greeted += [flipped]
+    greeted += [flip_to, flip_back]
     for to in greeted:
         pl.semaphore_signal(bar, inc=1, device_id=to)
 
@@ -153,56 +160,80 @@
     def bulk_gather_1(n, g):
         half, quart = place(g % 2, y)
         piece = B[n].at[g, 2 * half + quart, hl, hk]
-        return [
-            send(piece, piece, n + "_g1", (g, j - 1), dev(h=(h + j) % 4))
-            for j in (1, 2, 3)
-        ]
+        first, second = partners(g % 2, y)
+        z = {
+            j: send(piece, piece, n + "_g1", (g, j - 1), dev(h=(h + j) % 4))
+            for j in (1, 3, 2)
+        }
+        y2 = {0: send(piece, piece, n + "_g2", (g, 0), dev(y=second))}
+        y1 = {0: send(piece, piece, n + "_g3", (g, 0), dev(y=first))}
+        return z, y2, y1
 
     def bulk_gather_2(n, g, cps):
-        for cp in cps:
-            cp.wait_recv()
-        half, quart = place(g % 2, y)
-        piece = B[n].at[g, 2 * half + quart]
-        return send(piece, piece, n + "_g2", (g,), dev(y=partners(g % 2, y)[1]))
-
-    def bulk_gather_3(n, g, cp):
-        cp.wait_recv()
-        half, _ = place(g % 2, y)
-        piece = B[n].at[g, pl.ds(2 * half, 2)]
-        return send(piece, piece, n + "_g3", (g,), dev(y=partners(g % 2, y)[0]))
+        z, y2, y1 = cps
+        half, quart = place(g % 2, y)
+        first, second = partners(g % 2, y)
+        for j in (1, 3, 2):
+            z[j].wait_recv()
+            at = (h - j + 4) % 4
+            piece = B[n].at[g, 2 * half + quart, at // 2, at % 2]
+            y2[j] = send(piece, piece, n + "_g2", (g, j), dev(y=second))
+            y1[j] = send(piece, piece, n + "_g3", (g, j), dev(y=first))
+
+    def bulk_gather_3(n, g, cps, which):
+        _, y2, y1 = cps
+        half, quart = place(g % 2, y)
+        first, _ = partners(g % 2, y)
+        for j in which:
+            y2[j].wait_recv()
+            at = (h - j + 4) % 4
+            piece = B[n].at[g, 2 * half + 1 - quart, at // 2, at % 2]
+            y1[4 + j] = send(piece, piece, n + "_g3", (g, 4 + j), dev(y=first))
+
+    def bulk_gather_end(cps):
+        for j in range(8):
+            cps[2][j].wait_recv()
+
+    plain = (x, l, k, lambda at: at)
+    turned = (v, ul, uk, lambda at: (y - at + 4) % 4)
+    spot = {"fu": plain, "fr": turned}
 
     def col_sum_1(n, g):
+        _, _, sk, _ = spot[n]
         return send(
-            B[n].at[g, :, :, 1 - k], B[n + "_r1"].at[g], n + "_1", (g,), dev(k=1 - k)
+            B[n].at[g, :, :, 1 - sk], B[n + "_r1"].at[g], n + "_1", (g,), dev(k=1 - k)
         )
 
     def col_sum_2(n, g, cp):
         cp.wait_recv()
-        half, _ = place(g % 2, x)
+        sx, _, sk, ring = spot[n]
+        half, _ = place(g % 2, sx)
         f, r1, away = B[n], B[n + "_r1"], pl.ds(2 * (1 - half), 2)
-        out = f[g, away, :, k] + r1[g, away]
+        out = f[g, away, :, sk] + r1[g, away]
         B[n + "_s2"][g] = out.astype(B[n + "_s2"].dtype)
-        to = dev(x=partners(g % 2, x)[0])
+        to = dev(x=ring(partners(g % 2, sx)[0]))
         cp = send(B[n + "_s2"].at[g], B[n + "_r2"].at[g], n + "_2", (g,), to)
         here = pl.ds(2 * half, 2)
-        B[n + "_h"][g] = f[g, here, :, k] + r1[g, here]
+        B[n + "_h"][g] = f[g, here, :, sk] + r1[g, here]
         return cp
 
     def col_sum_3(n, g, cp):
         cp.wait_recv()
-        _, quart = place(g % 2, x)
+        sx, _, _, ring = spot[n]
+        _, quart = place(g % 2, sx)
         f, r2 = B[n + "_h"], B[n + "_r2"]
         out = f[g, 1 - quart] + r2[g, 1 - quart].astype(F32)
         B[n + "_s3"][g] = out.astype(B[n + "_s3"].dtype)
-        to = dev(x=partners(g % 2, x)[1])
+        to = dev(x=ring(partners(g % 2, sx)[1]))
         cp = send(B[n + "_s3"].at[g], B[n + "_r3"].at[g], n + "_3", (g,), to)
         B[n + "_q"][g] = f[g, quart] + r2[g, quart].astype(F32)
         return cp
 
     def col_sum_4(n, g, cp):
         cp.wait_recv()
+        sl = spot[n][1]
         f, r3 = B[n + "_q"], B[n + "_r3"]
-        out = f[g, 1 - l] + r3[g, 1 - l].astype(F32)
+        out = f[g, 1 - sl] + r3[g, 1 - sl].astype(F32)
         B[n + "_s4"][g] = out.astype(B[n + "_s4"].dtype)
         return send(
             B[n + "_s4"].at[g], B[n + "_r4"].at[g], n + "_4", (g,), dev(l=1 - l)
@@ -210,55 +241,72 @@
 
     def col_sum_end(n, g, cp):
         cp.wait_recv()
+        sl = spot[n][1]
         f, r3 = B[n + "_q"], B[n + "_r3"]
-        return f[g, l] + r3[g, l].astype(F32) + B[n + "_r4"][g].astype(F32)
-
-    def flip(src, dst, sem, g):
+        return f[g, sl] + r3[g, sl].astype(F32) + B[n + "_r4"][g].astype(F32)
+
+    def flip(src, dst, sem, g, to):
         cp = pltpu.make_async_remote_copy(
             src_ref=src,
             dst_ref=dst,
             send_sem=S[sem].at[0, g],
             recv_sem=S[sem].at[1, g],
-            device_id=flipped,
-        )
-
-        @pl.when(b != c)
+            device_id=to,
+        )
+
+        @pl.when(jnp.logical_not(fixed))
         def _():
             cp.start()
 
-        @pl.when(b == c)
+        @pl.when(fixed)
         def _():
             dst[...] = src[...]
 
+        pending_flips.append(cp)
         return cp
 
     def flip_wait(cp):
-        @pl.when(b != c)
+        @pl.when(jnp.logical_not(fixed))
         def _():
-            cp.wait()
+            cp.wait_recv()
+
+    def col_piece(n, g, dx, dl):
+        half, quart = place(g % 2, (v + dx) % 4)
+        low = ul if dl == 0 else 1 - ul
+        return B[n].at[g, 2 * half + quart, low, uk]
+
+    def col_across(n, g, i, piece):
+        return send(piece, piece, n + "_g3", (g, i), dev(k=1 - k))
+
+    def col_spread(n, g, dl):
+        piece = col_piece(n, g, 0, dl)
+        out = {
+            (dx, dl): send(piece, piece, n + "_g2", (g, 3 * dl + dx - 1), dev(x=(x + dx) % 4))
+            for dx in (1, 3, 2)
+        }
+        return out, [col_across(n, g, 4 * dl, piece)]
 
     def col_gather_1(n, g, cp):
         flip_wait(cp)
-        half, quart = place(g % 2, x)
-        piece = B[n].at[g, 2 * half + quart, l, k]
-        return send(piece, piece, n + "_g1", (g,), dev(l=1 - l))
-
-    def col_gather_2(n, g, cp):
-        cp.wait_recv()
-        half, quart = place(g % 2, x)
-        piece = B[n].at[g, 2 * half + quart, :, k]
-        return send(piece, piece, n + "_g2", (g,), dev(x=partners(g % 2, x)[1]))
-
-    def col_gather_3(n, g, cp):
-        cp.wait_recv()
-        half, _ = place(g % 2, x)
-        piece = B[n].at[g, pl.ds(2 * half, 2), :, k]
-        return send(piece, piece, n + "_g3", (g,), dev(x=partners(g % 2, x)[0]))
-
-    def col_gather_4(n, g, cp):
-        cp.wait_recv()
-        piece = B[n].at[g, :, :, k]
-        return send(piece, piece, n + "_g4", (g,), dev(k=1 - k))
+        piece = col_piece(n, g, 0, 0)
+        beside = send(piece, piece, n + "_g1", (g,), dev(l=1 - l))
+        return beside, *col_spread(n, g, 0)
+
+    def col_gather_2(n, g, cps):
+        beside, out, over = cps
+        beside.wait_recv()
+        more, too = col_spread(n, g, 1)
+        return {**out, **more}, over + too
+
+    def col_gather_3(n, g, cps, dl):
+        out, over = cps
+        for dx in (1, 3, 2):
+            out[dx, dl].wait_recv()
+            over.append(col_across(n, g, 4 * dl + dx, col_piece(n, g, dx, dl)))
+
+    def col_gather_end(cps):
+        for one in cps[1]:
+            one.wait_recv()
 
     groups = range(GROUPS)
     of_chunk = [(2 * p, 2 * p + 1) for p in range(CHUNKS)]
@@ -284,62 +332,69 @@
         half, quart = place(g % 2, y)
         at = (g, 2 * half + quart, hl, hk)
         B["pc"][at] = bulk_sum_end("fp", g, cp[g]).astype(BF)
+        far[g] = flip(B["pc"].at[at], B["pr"].at[at], "pr_t", g, flip_to)
+    for g in groups:
         near[g] = bulk_gather_1("pc", g)
-        far[g] = flip(B["pc"].at[at], B["pr"].at[at], "pr_t", g)
-
+
+    for g in groups:
+        bulk_gather_3("pc", g, near[g], (0,))
     for g in groups:
         far[g] = col_gather_1("pr", g, far[g])
     for g in groups:
-        near[g] = bulk_gather_2("pc", g, near[g])
+        bulk_gather_2("pc", g, near[g])
     for g in groups:
         far[g] = col_gather_2("pr", g, far[g])
     for g in groups:
-        near[g] = bulk_gather_3("pc", g, near[g])
-    for g in groups:
-        far[g] = col_gather_3("pr", g, far[g])
-    for g in groups:
-        far[g] = col_gather_4("pr", g, far[g])
+        col_gather_3("pr", g, far[g], 0)
+    for g in groups:
+        bulk_gather_3("pc", g, near[g], (1, 3, 2))
+    for g in groups:
+        col_gather_3("pr", g, far[g], 1)
+
     row, col = {}, {}
     for p in range(CHUNKS):
         for g in of_chunk[p]:
-            near[g].wait_recv()
+            bulk_gather_end(near[g])
         split_rows("fr", p, dot(B["mx"][...], joined("pc", p), 1, 0), 64)
         for g in of_chunk[p]:
             row[g] = col_sum_1("fr", g)
-        for g in of_chunk[p]:
-            far[g].wait_recv()
+    for p in range(CHUNKS):
+        for g in of_chunk[p]:
+            col_gather_end(far[g])
         split_rows("fc", p, dot(B["mx"][...], joined("pr", p), 0, 0), 64)
         for g in of_chunk[p]:
             col[g] = bulk_sum_1("fc", g)
-
-    for g in groups:
-        row[g] = col_sum_2("fr", g, row[g])
+        for g in of_chunk[p]:
+            row[g] = col_sum_2("fr", g, row[g])
+    for g in groups:
+        row[g] = col_sum_3("fr", g, row[g])
     for g in groups:
         col[g] = bulk_sum_2("fc", g, col[g])
     for g in groups:
-        row[g] = col_sum_3("fr", g, row[g])
+        row[g] = col_sum_4("fr", g, row[g])
+    for g in groups:
+        B["fr_t"][g] = col_sum_end("fr", g, row[g]).astype(BF)
+        row[g] = flip(B["fr_t"].at[g], B["fr_u"].at[g], "fr_t", g, flip_back)
     for g in groups:
         col[g] = bulk_sum_3("fc", g, col[g])
-    for g in groups:
-        row[g] = col_sum_4("fr", g, row[g])
-    for g in groups:
-        B["fr_t"][g] = col_sum_end("fr", g, row[g])
-        row[g] = flip(B["fr_t"].at[g], B["fr_u"].at[g], "fr_t", g)
     for g in groups:
         total = bulk_sum_end("fc", g, col[g])
         flip_wait(row[g])
-        half, quart = place(g % 2, y)
-        rotated = (0.5 * (total + B["fr_u"][g])).astype(BF)
+        total = total + B["fr_u"][g].astype(F32)
+        half, quart = place(g % 2, y)
+        rotated = (0.5 * total).astype(BF)
         B["ro"][g, 2 * half + quart, hl, hk] = rotated
         near[g] = bulk_gather_1("ro", g)
     for g in groups:
-        near[g] = bulk_gather_2("ro", g, near[g])
-    for g in groups:
-        near[g] = bulk_gather_3("ro", g, near[g])
+        bulk_gather_3("ro", g, near[g], (0,))
+    for g in groups:
+        bulk_gather_2("ro", g, near[g])
+    for g in groups:
+        bulk_gather_3("ro", g, near[g], (1, 3, 2))
 
     for p in range(CHUNKS):
         for g in of_chunk[p]:
-            near[g].wait_recv()
+            bulk_gather_end(near[g])
         value = dot(B["co"][...], joined("ro", p), 1, 0)
         for g in of_chunk[p]:
             i = g % 2
@@ -357,6 +412,11 @@
         o_ref[:, g * LANES : (g + 1) * LANES] = col_sum_end("fu", g, row[g])
     for one in pending:
         one.wait_send()
+
+    @pl.when(jnp.logical_not(fixed))
+    def _():
+        for one in pending_flips:
+            one.wait_send()
 
 
 def scratch():
@@ -374,18 +434,18 @@
             n + "_own": V((GROUPS, 64, LANES), F32),
         }
 
-    def col(n, rows, two, three, four):
+    def col(n, rows, t, last):
         return {
             n: V((GROUPS, 4, 2, 2, rows, LANES), F32),
             n + "_r1": V((GROUPS, 4, 2, rows, LANES), F32),
             n + "_h": V((GROUPS, 2, 2, rows, LANES), F32),
-            n + "_s2": V((GROUPS, 2, 2, rows, LANES), two),
-            n + "_r2": V((GROUPS, 2, 2, rows, LANES), two),
+            n + "_s2": V((GROUPS, 2, 2, rows, LANES), t),
+            n + "_r2": V((GROUPS, 2, 2, rows, LANES), t),
             n + "_q": V((GROUPS, 2, rows, LANES), F32),
-            n + "_s3": V((GROUPS, 2, rows, LANES), three),
-            n + "_r3": V((GROUPS, 2, rows, LANES), three),
-            n + "_s4": V((GROUPS, rows, LANES), four),
-            n + "_r4": V((GROUPS, rows, LANES), four),
+            n + "_s3": V((GROUPS, 2, rows, LANES), t),
+            n + "_r3": V((GROUPS, 2, rows, LANES), t),
+            n + "_s4": V((GROUPS, rows, LANES), last),
+            n + "_r4": V((GROUPS, rows, LANES), last),
         }
 
     whole = (GROUPS, 4, 2, 2, 64, LANES)
@@ -398,12 +458,12 @@
         "pc": V(whole, BF),
         "pr": V(whole, BF),
         "ro": V(whole, BF),
-        "fr_t": V((GROUPS, 64, LANES), F32),
-        "fr_u": V((GROUPS, 64, LANES), F32),
+        "fr_t": V((GROUPS, 64, LANES), BF),
+        "fr_u": V((GROUPS, 64, LANES), BF),
         **bulk("fp", BF),
         **bulk("fc", BF),
-        **col("fr", 64, F32, F32, F32),
-        **col("fu", 96, BF, BF, BF),
+        **col("fr", 64, BF, F32),
+        **col("fu", 96, BF, BF),
     }
     D = pltpu.SemaphoreType.DMA
     sems = {"load": D((3,)), "a": D((2, CHUNKS, 7)), "ac": D((2, CHUNKS, 8))}
@@ -411,13 +471,14 @@
         sems.update({n + "_1": D((2, GROUPS)), n + "_2": D((2, GROUPS))})
         sems[n + "_3"] = D((2, GROUPS, 3))
     for n in ("pc", "ro"):
-        sems.update({n + "_g2": D((2, GROUPS)), n + "_g3": D((2, GROUPS))})
+        sems.update({n + "_g2": D((2, GROUPS, 4)), n + "_g3": D((2, GROUPS, 8))})
         sems[n + "_g1"] = D((2, GROUPS, 3))
     for i in range(1, 5):
-        for n in ("fr_", "fu_", "pr_g"):
+        for n in ("fr_", "fu_"):
             sems[n + str(i)] = D((2, GROUPS))
-    sems["pr_t"] = D((2, GROUPS))
-    sems["fr_t"] = D((2, GROUPS))
+    for n in ("pr_g1", "pr_t", "fr_t"):
+        sems[n] = D((2, GROUPS))
+    sems.update({"pr_g2": D((2, GROUPS, 6)), "pr_g3": D((2, GROUPS, 8))})
     return bufs, sems
 
 

time: 125 us -> 118 us (0.944)
  Pallas kernels: 124 us -> 116 us
    pallas_call x1, Pallas kernels: 124 us -> 116 us  [shards(): pl.pallas_call(body, out_shape=jax.ShapeDtypeStruct(s_half.shape, F32), i...]
where the time goes in v2:
time: 118 us
  Pallas kernels  116 us (98%)
  local copies, waits for them, and re-layouts  1.62 us (1%)
    pallas_call x1, Pallas kernels, shards(): pl.pallas_call(body, out_shape=jax.ShapeDtypeStruct(s_half.shape, F32), i...  116 us

profile of v2, /device:TPU:1, one launch (start us, length us, event | category | flops | bytes accessed | tf_op | source)
XLA Modules:
  0.0 117.8 jit_solution(14710055102010480545)
XLA Ops:
  0.0 116.2 %gw_update.1 = f32[96,512]{1,0:T(8,128)} custom-call(bf16[1024,1024]{1,0:T(8,128)(2,1)} %refs_0_.1, bf16[1024,1024]{1,0:T(8,128)(2,1)} %refs_1_.1, bf16[1536,1024]{1,0:T(8,128)(2,1)} %refs_2_.1, bf16[96,512]{1,0:T(8,128)(2,1)} %refs_3_.1), custom_call_target="tpu_custom_call" | custom-call | tf_op jit(solution)/shard_map/gw_update/pallas_call | solution.py:498
  116.2 1.6 %copy.6 = f32[96,512]{1,0:T(8,128)} copy(f32[96,512]{1,0:T(8,128)} %gw_update.1) | data formatting | bytes 393216

commit v3 on v2

--- a/solution.py
+++ b/solution.py
@@ -102,10 +102,15 @@
     lax.fori_loop(0, 16, mix, 0)
     loads[2].wait()
 
-    def split_rows(name, p, value, rows):
-        for i in range(2):
-            part = value[:, i * LANES : (i + 1) * LANES]
-            B[name][2 * p + i] = part.reshape(4, 2, 2, rows, LANES)
+    def multiply(name, p, left, da, right, rows):
+        for q in range(4):
+            r = slice(4 * rows * q, 4 * rows * (q + 1))
+            part = B[left][:, r] if da == 0 else B[left][r, :]
+            value = dot(part, right, da, 0)
+            for i in range(2):
+                slot = SLOTS[i][q] if name == "fu" else q
+                tile = value[:, i * LANES : (i + 1) * LANES]
+                B[name][2 * p + i, slot] = tile.reshape(2, 2, rows, LANES)
 
     def joined(name, p):
         return jnp.concatenate(
@@ -194,6 +199,27 @@
         for j in range(8):
             cps[2][j].wait_recv()
 
+    def row_sum_2(g, cp):
+        cp.wait_recv()
+        total = B["fr"][g, :, :, uk] + B["fr_r1"][g]
+        B["fr_h"][g] = total
+        B["fr_s2"][g] = total.astype(BF)
+        cps = []
+        for i, (dx, dl) in enumerate(shifts):
+            half, quart = place(g % 2, (v - dx + 4) % 4)
+            low = 1 - ul if dl else ul
+            piece = B["fr_s2"].at[g, 2 * half + quart, low]
+            cps.append(send(piece, B["fr_r2"].at[g, i], "fr_2", (g, i), peers[i]))
+        return cps
+
+    def row_sum_end(g, cps):
+        half, quart = place(g % 2, v)
+        total = B["fr_h"][g, 2 * half + quart, ul]
+        for i, one in enumerate(cps):
+            one.wait_recv()
+            total = total + B["fr_r2"][g, i].astype(F32)
+        return total
+
     plain = (x, l, k, lambda at: at)
     turned = (v, ul, uk, lambda at: (y - at + 4) % 4)
     spot = {"fu": plain, "fr": turned}
@@ -320,7 +346,7 @@
         for one in across[p]:
             one.wait_recv()
         rows = B["sg"][p].reshape(-1, 2 * LANES)
-        split_rows("fp", p, dot(B["co"][...], rows, 0, 0), 64)
+        multiply("fp", p, "co", 0, rows, 64)
         for g in of_chunk[p]:
             cp[g] = bulk_sum_1("fp", g)
     for g in groups:
@@ -355,25 +381,21 @@
     for p in range(CHUNKS):
         for g in of_chunk[p]:
             bulk_gather_end(near[g])
-        split_rows("fr", p, dot(B["mx"][...], joined("pc", p), 1, 0), 64)
+        multiply("fr", p, "mx", 1, joined("pc", p), 64)
         for g in of_chunk[p]:
             row[g] = col_sum_1("fr", g)
     for p in range(CHUNKS):
         for g in of_chunk[p]:
             col_gather_end(far[g])
-        split_rows("fc", p, dot(B["mx"][...], joined("pr", p), 0, 0), 64)
+        multiply("fc", p, "mx", 0, joined("pr", p), 64)
         for g in of_chunk[p]:
             col[g] = bulk_sum_1("fc", g)
         for g in of_chunk[p]:
-            row[g] = col_sum_2("fr", g, row[g])
-    for g in groups:
-        row[g] = col_sum_3("fr", g, row[g])
+            row[g] = row_sum_2(g, row[g])
     for g in groups:
         col[g] = bulk_sum_2("fc", g, col[g])
     for g in groups:
-        row[g] = col_sum_4("fr", g, row[g])
-    for g in groups:
-        B["fr_t"][g] = col_sum_end("fr", g, row[g]).astype(BF)
+        B["fr_t"][g] = row_sum_end(g, row[g]).astype(BF)
         row[g] = flip(B["fr_t"].at[g], B["fr_u"].at[g], "fr_t", g, flip_back)
     for g in groups:
         col[g] = bulk_sum_3("fc", g, col[g])
@@ -395,12 +417,8 @@
     for p in range(CHUNKS):
         for g in of_chunk[p]:
             bulk_gather_end(near[g])
-        value = dot(B["co"][...], joined("ro", p), 1, 0)
-        for g in of_chunk[p]:
-            i = g % 2
-            part = value[:, i * LANES : (i + 1) * LANES].reshape(4, 2, 2, 96, LANES)
-            for v in range(4):
-                B["fu"][g, SLOTS[i][v]] = part[v]
+        multiply("fu", p, "co", 1, joined("ro", p), 96)
+        for g in of_chunk[p]:
             row[g] = col_sum_1("fu", g)
     for g in groups:
         row[g] = col_sum_2("fu", g, row[g])
@@ -462,7 +480,11 @@
         "fr_u": V((GROUPS, 64, LANES), BF),
         **bulk("fp", BF),
         **bulk("fc", BF),
-        **col("fr", 64, BF, F32),
+        "fr": V(whole, F32),
+        "fr_r1": V((GROUPS, 4, 2, 64, LANES), F32),
+        "fr_h": V((GROUPS, 4, 2, 64, LANES), F32),
+        "fr_s2": V((GROUPS, 4, 2, 64, LANES), BF),
+        "fr_r2": V((GROUPS, 7, 64, LANES), BF),
         **col("fu", 96, BF, BF),
     }
     D = pltpu.SemaphoreType.DMA
@@ -474,9 +496,9 @@
         sems.update({n + "_g2": D((2, GROUPS, 4)), n + "_g3": D((2, GROUPS, 8))})
         sems[n + "_g1"] = D((2, GROUPS, 3))
     for i in range(1, 5):
-        for n in ("fr_", "fu_"):
-            sems[n + str(i)] = D((2, GROUPS))
-    for n in ("pr_g1", "pr_t", "fr_t"):
+        sems["fu_" + str(i)] = D((2, GROUPS))
+    sems["fr_2"] = D((2, GROUPS, 7))
+    for n in ("pr_g1", "pr_t", "fr_t", "fr_1"):
         sems[n] = D((2, GROUPS))
     sems.update({"pr_g2": D((2, GROUPS, 6)), "pr_g3": D((2, GROUPS, 8))})
     return bufs, sems

time: 118 us -> 114 us (0.966)
  Pallas kernels: 116 us -> 112 us
    pallas_call x1, Pallas kernels: 116 us -> 112 us  [shards(): pl.pallas_call(body, out_shape=jax.ShapeDtypeStruct(s_half.shape, F32), i...]
where the time goes in v3:
time: 114 us; the launch traced here: 113 us
  Pallas kernels  112 us (98%)
  local copies, waits for them, and re-layouts  1.62 us (1%)
    pallas_call x1, Pallas kernels, shards(): pl.pallas_call(body, out_shape=jax.ShapeDtypeStruct(s_half.shape, F32), i...  112 us

profile of v3, /device:TPU:1, one launch (start us, length us, event | category | flops | bytes accessed | tf_op | source)
XLA Modules:
  0.0 113.5 jit_solution(15824405891460961078)
XLA Ops:
  0.0 111.8 %gw_update.1 = f32[96,512]{1,0:T(8,128)} custom-call(bf16[1024,1024]{1,0:T(8,128)(2,1)} %refs_0_.1, bf16[1024,1024]{1,0:T(8,128)(2,1)} %refs_1_.1, bf16[1536,1024]{1,0:T(8,128)(2,1)} %refs_2_.1, bf16[96,512]{1,0:T(8,128)(2,1)} %refs_3_.1), custom_call_target="tpu_custom_call" | custom-call | tf_op jit(solution)/shard_map/gw_update/pallas_call | solution.py:520
  111.9 1.6 %copy.6 = f32[96,512]{1,0:T(8,128)} copy(f32[96,512]{1,0:T(8,128)} %gw_update.1) | data formatting | bytes 393216

commit v4 on v3

--- a/solution.py
+++ b/solution.py
@@ -199,77 +199,34 @@
         for j in range(8):
             cps[2][j].wait_recv()
 
-    def row_sum_2(g, cp):
+    def col_sum_2(n, g, cp):
         cp.wait_recv()
-        total = B["fr"][g, :, :, uk] + B["fr_r1"][g]
-        B["fr_h"][g] = total
-        B["fr_s2"][g] = total.astype(BF)
+        sx, sl, sk, sign = spot[n]
+        total = B[n][g, :, :, sk] + B[n + "_r1"][g].astype(F32)
+        B[n + "_h"][g] = total
+        B[n + "_s2"][g] = total.astype(BF)
         cps = []
         for i, (dx, dl) in enumerate(shifts):
-            half, quart = place(g % 2, (v - dx + 4) % 4)
-            low = 1 - ul if dl else ul
-            piece = B["fr_s2"].at[g, 2 * half + quart, low]
-            cps.append(send(piece, B["fr_r2"].at[g, i], "fr_2", (g, i), peers[i]))
+            half, quart = place(g % 2, (sx + sign * dx + 4) % 4)
+            piece = B[n + "_s2"].at[g, 2 * half + quart, 1 - sl if dl else sl]
+            cps.append(send(piece, B[n + "_r2"].at[g, i], n + "_2", (g, i), peers[i]))
         return cps
 
-    def row_sum_end(g, cps):
-        half, quart = place(g % 2, v)
-        total = B["fr_h"][g, 2 * half + quart, ul]
+    def col_sum_end(n, g, cps):
+        sx, sl, _, _ = spot[n]
+        half, quart = place(g % 2, sx)
+        total = B[n + "_h"][g, 2 * half + quart, sl]
         for i, one in enumerate(cps):
             one.wait_recv()
-            total = total + B["fr_r2"][g, i].astype(F32)
+            total = total + B[n + "_r2"][g, i].astype(F32)
         return total
 
-    plain = (x, l, k, lambda at: at)
-    turned = (v, ul, uk, lambda at: (y - at + 4) % 4)
-    spot = {"fu": plain, "fr": turned}
+    spot = {"fu": (x, l, k, 1), "fr": (v, ul, uk, -1)}
 
     def col_sum_1(n, g):
-        _, _, sk, _ = spot[n]
-        return send(
-            B[n].at[g, :, :, 1 - sk], B[n + "_r1"].at[g], n + "_1", (g,), dev(k=1 - k)
-        )
-
-    def col_sum_2(n, g, cp):
-        cp.wait_recv()
-        sx, _, sk, ring = spot[n]
-        half, _ = place(g % 2, sx)
-        f, r1, away = B[n], B[n + "_r1"], pl.ds(2 * (1 - half), 2)
-        out = f[g, away, :, sk] + r1[g, away]
-        B[n + "_s2"][g] = out.astype(B[n + "_s2"].dtype)
-        to = dev(x=ring(partners(g % 2, sx)[0]))
-        cp = send(B[n + "_s2"].at[g], B[n + "_r2"].at[g], n + "_2", (g,), to)
-        here = pl.ds(2 * half, 2)
-        B[n + "_h"][g] = f[g, here, :, sk] + r1[g, here]
-        return cp
-
-    def col_sum_3(n, g, cp):
-        cp.wait_recv()
-        sx, _, _, ring = spot[n]
-        _, quart = place(g % 2, sx)
-        f, r2 = B[n + "_h"], B[n + "_r2"]
-        out = f[g, 1 - quart] + r2[g, 1 - quart].astype(F32)
-        B[n + "_s3"][g] = out.astype(B[n + "_s3"].dtype)
-        to = dev(x=ring(partners(g % 2, sx)[1]))
-        cp = send(B[n + "_s3"].at[g], B[n + "_r3"].at[g], n + "_3", (g,), to)
-        B[n + "_q"][g] = f[g, quart] + r2[g, quart].astype(F32)
-        return cp
-
-    def col_sum_4(n, g, cp):
-        cp.wait_recv()
-        sl = spot[n][1]
-        f, r3 = B[n + "_q"], B[n + "_r3"]
-        out = f[g, 1 - sl] + r3[g, 1 - sl].astype(F32)
-        B[n + "_s4"][g] = out.astype(B[n + "_s4"].dtype)
-        return send(
-            B[n + "_s4"].at[g], B[n + "_r4"].at[g], n + "_4", (g,), dev(l=1 - l)
-        )
-
-    def col_sum_end(n, g, cp):
-        cp.wait_recv()
-        sl = spot[n][1]
-        f, r3 = B[n + "_q"], B[n + "_r3"]
-        return f[g, sl] + r3[g, sl].astype(F32) + B[n + "_r4"][g].astype(F32)
+        away = 1 - spot[n][2]
+        src = B[n].at[g, :, :, away]
+        return send(src, B[n + "_r1"].at[g], n + "_1", (g,), dev(k=1 - k))
 
     def flip(src, dst, sem, g, to):
         cp = pltpu.make_async_remote_copy(
@@ -384,18 +341,18 @@
         multiply("fr", p, "mx", 1, joined("pc", p), 64)
         for g in of_chunk[p]:
             row[g] = col_sum_1("fr", g)
+    for g in groups:
+        row[g] = col_sum_2("fr", g, row[g])
     for p in range(CHUNKS):
         for g in of_chunk[p]:
             col_gather_end(far[g])
         multiply("fc", p, "mx", 0, joined("pr", p), 64)
         for g in of_chunk[p]:
             col[g] = bulk_sum_1("fc", g)
-        for g in of_chunk[p]:
-            row[g] = row_sum_2(g, row[g])
     for g in groups:
         col[g] = bulk_sum_2("fc", g, col[g])
     for g in groups:
-        B["fr_t"][g] = row_sum_end(g, row[g]).astype(BF)
+        B["fr_t"][g] = col_sum_end("fr", g, row[g]).astype(BF)
         row[g] = flip(B["fr_t"].at[g], B["fr_u"].at[g], "fr_t", g, flip_back)
     for g in groups:
         col[g] = bulk_sum_3("fc", g, col[g])
@@ -422,10 +379,6 @@
             row[g] = col_sum_1("fu", g)
     for g in groups:
         row[g] = col_sum_2("fu", g, row[g])
-    for g in groups:
-        row[g] = col_sum_3("fu", g, row[g])
-    for g in groups:
-        row[g] = col_sum_4("fu", g, row[g])
     for g in groups:
         o_ref[:, g * LANES : (g + 1) * LANES] = col_sum_end("fu", g, row[g])
     for one in pending:
@@ -452,18 +405,14 @@
             n + "_own": V((GROUPS, 64, LANES), F32),
         }
 
-    def col(n, rows, t, last):
+    def col(n, rows, t):
         return {
             n: V((GROUPS, 4, 2, 2, rows, LANES), F32),
-            n + "_r1": V((GROUPS, 4, 2, rows, LANES), F32),
-            n + "_h": V((GROUPS, 2, 2, rows, LANES), F32),
-            n + "_s2": V((GROUPS, 2, 2, rows, LANES), t),
-            n + "_r2": V((GROUPS, 2, 2, rows, LANES), t),
-            n + "_q": V((GROUPS, 2, rows, LANES), F32),
-            n + "_s3": V((GROUPS, 2, rows, LANES), t),
-            n + "_r3": V((GROUPS, 2, rows, LANES), t),
-            n + "_s4": V((GROUPS, rows, LANES), last),
-            n + "_r4": V((GROUPS, rows, LANES), last),
+            n + "_s1": V((GROUPS, 4, 2, rows, LANES), t),
+            n + "_r1": V((GROUPS, 4, 2, rows, LANES), t),
+            n + "_h": V((GROUPS, 4, 2, rows, LANES), F32),
+            n + "_s2": V((GROUPS, 4, 2, rows, LANES), BF),
+            n + "_r2": V((GROUPS, 7, rows, LANES), BF),
         }
 
     whole = (GROUPS, 4, 2, 2, 64, LANES)
@@ -480,12 +429,8 @@
         "fr_u": V((GROUPS, 64, LANES), BF),
         **bulk("fp", BF),
         **bulk("fc", BF),
-        "fr": V(whole, F32),
-        "fr_r1": V((GROUPS, 4, 2, 64, LANES), F32),
-        "fr_h": V((GROUPS, 4, 2, 64, LANES), F32),
-        "fr_s2": V((GROUPS, 4, 2, 64, LANES), BF),
-        "fr_r2": V((GROUPS, 7, 64, LANES), BF),
-        **col("fu", 96, BF, BF),
+        **col("fr", 64, F32),
+        **col("fu", 96, F32),
     }
     D = pltpu.SemaphoreType.DMA
     sems = {"load": D((3,)), "a": D((2, CHUNKS, 7)), "ac": D((2, CHUNKS, 8))}
@@ -495,10 +440,9 @@
     for n in ("pc", "ro"):
         sems.update({n + "_g2": D((2, GROUPS, 4)), n + "_g3": D((2, GROUPS, 8))})
         sems[n + "_g1"] = D((2, GROUPS, 3))
-    for i in range(1, 5):
-        sems["fu_" + str(i)] = D((2, GROUPS))
     sems["fr_2"] = D((2, GROUPS, 7))
-    for n in ("pr_g1", "pr_t", "fr_t", "fr_1"):
+    sems["fu_2"] = D((2, GROUPS, 7))
+    for n in ("pr_g1", "pr_t", "fr_t", "fr_1", "fu_1"):
         sems[n] = D((2, GROUPS))
     sems.update({"pr_g2": D((2, GROUPS, 6)), "pr_g3": D((2, GROUPS, 8))})
     return bufs, sems

time: 114 us -> 111 us (0.974)
  Pallas kernels: 112 us -> 109 us
    pallas_call x1, Pallas kernels: 112 us -> 109 us  [shards(): pl.pallas_call(body, out_shape=jax.ShapeDtypeStruct(s_half.shape, F32), i...]
where the time goes in v4:
time: 111 us
  Pallas kernels  109 us (98%)
  local copies, waits for them, and re-layouts  1.62 us (1%)
    pallas_call x1, Pallas kernels, shards(): pl.pallas_call(body, out_shape=jax.ShapeDtypeStruct(s_half.shape, F32), i...  109 us

profile of v4, /device:TPU:1, one launch (start us, length us, event | category | flops | bytes accessed | tf_op | source)
XLA Modules:
  0.0 111.0 jit_solution(2400143839387376375)
XLA Ops:
  0.0 109.4 %gw_update.1 = f32[96,512]{1,0:T(8,128)} custom-call(bf16[1024,1024]{1,0:T(8,128)(2,1)} %refs_0_.1, bf16[1024,1024]{1,0:T(8,128)(2,1)} %refs_1_.1, bf16[1536,1024]{1,0:T(8,128)(2,1)} %refs_2_.1, bf16[96,512]{1,0:T(8,128)(2,1)} %refs_3_.1), custom_call_target="tpu_custom_call" | custom-call | tf_op jit(solution)/shard_map/gw_update/pallas_call | solution.py:464
  109.4 1.6 %copy.6 = f32[96,512]{1,0:T(8,128)} copy(f32[96,512]{1,0:T(8,128)} %gw_update.1) | data formatting | bytes 393216
